TPU v7x, 32 devices: a whole 2x2x4 slice. The times are simulated.
32 devices in a mesh: shard: 4 (over y, x), ctx: 8 (over z, core).
Axes of the slice: x: 2, y: 2, z: 4, core: 2. Of those that a mesh axis runs over, the one named last changes fastest.
Arguments:
- tokens: bfloat16 [4, 1024, 768], P('shard', 'ctx'), may hold values from -60 to 60
- lengths: int32 [4], P('shard'), may hold values from 128 to 1024, as said below
- cotangent: bfloat16 [4, 1024, 768], P('shard', 'ctx'), may hold values from -6 to 6
- w_qkv: bfloat16 [768, 2304], P('shard'), may hold values from -0.21875 to 0.21875
- b_query: bfloat16 [768], P('shard'), may hold values from -3 to 3
- b_value: bfloat16 [768], P('shard'), may hold values from -3 to 3
- w_out: bfloat16 [768, 768], P('shard'), may hold values from -3.5 to 3.5
- b_out: bfloat16 [768], P('shard'), may hold values from -3 to 3
- ln1_gain: bfloat16 [768], P('shard'), may hold values from 0.25 to 1.75
- ln1_bias: bfloat16 [768], P('shard'), may hold values from -3 to 3
- w_up: bfloat16 [768, 3072], P('shard'), may hold values from -0.21875 to 0.21875
- b_up: bfloat16 [3072], P('shard'), may hold values from -3 to 3
- w_down: bfloat16 [3072, 768], P('shard'), may hold values from -0.109375 to 0.109375
- b_down: bfloat16 [768], P('shard'), may hold values from -3 to 3
- ln2_gain: bfloat16 [768], P('shard'), may hold values from 0.25 to 1.75
- ln2_bias: bfloat16 [768], P('shard'), may hold values from -3 to 3
Outputs:
- output: bfloat16 [4, 1024, 768], P('shard', 'ctx')
- tokens_grad: float32 [4, 1024, 768], P('shard', 'ctx')
- w_qkv_grad: float32 [768, 2304], P('shard')
- b_query_grad: float32 [768], P('shard')
- b_value_grad: float32 [768], P('shard')
- w_out_grad: float32 [768, 768], P('shard')
- b_out_grad: float32 [768], P('shard')
- ln1_gain_grad: float32 [768], P('shard')
- ln1_bias_grad: float32 [768], P('shard')
- w_up_grad: float32 [768, 3072], P('shard')
- b_up_grad: float32 [3072], P('shard')
- w_down_grad: float32 [3072, 768], P('shard')
- b_down_grad: float32 [768], P('shard')
- ln2_gain_grad: float32 [768], P('shard')
- ln2_bias_grad: float32 [768], P('shard')
Inputs may be any that keep to these rules, and one draw needn't show every extreme that they name: `lengths`: each sequence has at least one valid token; some sequence is entirely valid.
All inputs are finite; a program needn't handle non-finite values.
Results may differ from a plain program's by a relative error of at most 0.035.
The roundings to bfloat16 on the way count: a program that leaves them out, or rounds other values in their place, can miss the bound.
Values may be sent and summed in bfloat16 or wider, within the bound.
A program may use at most 128 MiB of HBM per device.

v0:
```python
import math
import jax
import jax.numpy as jnp
from jax import lax
from jax.sharding import PartitionSpec as P

HEADS = 12
EPS = 1e-06


def normalize(z):
    centre = z - jnp.mean(z, axis=-1, keepdims=True)
    rstd = lax.rsqrt(jnp.mean(centre * centre, axis=-1, keepdims=True) + EPS)
    return (centre * rstd, rstd)


def norm_back(dnorm, normed, rstd):
    return rstd * (
        dnorm
        - jnp.mean(dnorm, axis=-1, keepdims=True)
        - normed * jnp.mean(dnorm * normed, axis=-1, keepdims=True)
    )


def gelu_exact(t):
    return jax.nn.gelu(t, approximate=False)


def contract_dims(left, right, left_dim, right_dim):
    return lax.dot_general(
        left, right, (((left_dim,), (right_dim,)), ((), ())), preferred_element_type=jnp.float32
    )


def heads_first(a):
    return a.reshape(HEADS, a.shape[0] // HEADS, a.shape[1])


def local(
    tokens,
    lengths,
    cotangent,
    w_qkv,
    b_query,
    b_value,
    w_out,
    b_out,
    ln1_gain,
    ln1_bias,
    w_up,
    b_up,
    w_down,
    b_down,
    ln2_gain,
    ln2_bias,
):
    single_float = jnp.float32
    bf16 = jnp.bfloat16
    full = (
        lax.all_gather(w_qkv, "shard", axis=0, tiled=True),
        lax.all_gather(b_query, "shard", axis=0, tiled=True),
        lax.all_gather(b_value, "shard", axis=0, tiled=True),
        lax.all_gather(w_out, "shard", axis=0, tiled=True),
        lax.all_gather(b_out, "shard", axis=0, tiled=True),
        lax.all_gather(ln1_gain, "shard", axis=0, tiled=True),
        lax.all_gather(ln1_bias, "shard", axis=0, tiled=True),
        lax.all_gather(w_up, "shard", axis=0, tiled=True),
        lax.all_gather(b_up, "shard", axis=0, tiled=True),
        lax.all_gather(w_down, "shard", axis=0, tiled=True),
        lax.all_gather(b_down, "shard", axis=0, tiled=True),
        lax.all_gather(ln2_gain, "shard", axis=0, tiled=True),
        lax.all_gather(ln2_bias, "shard", axis=0, tiled=True),
    )
    wq_full, wo_full, wu_full, wd_full = (full[0], full[3], full[7], full[9])
    bq, bv, bo = (
        full[1].astype(single_float),
        full[2].astype(single_float),
        full[4].astype(single_float),
    )
    g1, c1, bu = (
        full[5].astype(single_float),
        full[6].astype(single_float),
        full[8].astype(single_float),
    )
    bd, g2, c2 = (
        full[10].astype(single_float),
        full[11].astype(single_float),
        full[12].astype(single_float),
    )
    x = tokens[0]
    width = x.shape[1]
    head_size = width // HEADS
    scale = 1.0 / math.sqrt(head_size)
    limit = lengths[0]
    qkv_t = contract_dims(wq_full, x, 0, 1)
    query_t = (qkv_t[:width] + bq[:, None]).astype(bf16)
    keys_t = qkv_t[width : 2 * width].astype(bf16)
    values_t = (qkv_t[2 * width :] + bv[:, None]).astype(bf16)
    all_keys, all_values = (
        lax.all_gather(keys_t, "ctx", axis=1, tiled=True),
        lax.all_gather(values_t, "ctx", axis=1, tiled=True),
    )
    total = all_keys.shape[1]
    valid = jnp.arange(total, dtype=jnp.int32) < limit

    def head_fwd(operations):
        query_index, key_index, value_index = operations
        scores = contract_dims(query_index, key_index, 0, 0) * scale
        scores = jnp.where(valid[None, :], scores, -1e30)
        peak = jnp.max(scores, axis=1, keepdims=True)
        lse = peak + jnp.log(jnp.sum(jnp.exp(scores - peak), axis=1, keepdims=True))
        probs = jnp.exp(scores - lse).astype(bf16)
        return (contract_dims(value_index, probs, 1, 1), lse[:, 0])

    ctx_heads, lse_all = lax.map(
        head_fwd, (heads_first(query_t), heads_first(all_keys), heads_first(all_values))
    )
    context_b_t = ctx_heads.reshape(width, -1).astype(bf16)
    z_one = x.astype(single_float) + contract_dims(context_b_t, wo_full, 0, 0) + bo
    n_one, rstd_one = normalize(z_one)
    x_one = n_one * g1 + c1
    x_one_b = x_one.astype(bf16)
    upper = jnp.dot(x_one_b, wu_full, preferred_element_type=single_float) + bu
    hidden_f, gelu_back = jax.vjp(gelu_exact, upper)
    hidden = hidden_f.astype(bf16)
    z_two = x_one + jnp.dot(hidden, wd_full, preferred_element_type=single_float) + bd
    n_two, rstd_two = normalize(z_two)
    out = (n_two * g2 + c2).astype(bf16)
    wq_back, wo_back, wu_back, wd_back = (wq_full, wo_full, wu_full, wd_full)
    keys_b, values_b = (all_keys, all_values)
    grad = cotangent[0].astype(single_float)
    dg_two = jnp.sum(grad * n_two, axis=0)
    db_two = jnp.sum(grad, axis=0)
    dz_two = norm_back(grad * g2, n_two, rstd_two)
    dz_two_b = dz_two.astype(bf16)
    dw_down = contract_dims(hidden, dz_two_b, 0, 0)
    db_down = jnp.sum(dz_two, axis=0)
    dhid = contract_dims(dz_two_b, wd_back, 1, 1)
    dupper = gelu_back(dhid)[0]
    dupper_b = dupper.astype(bf16)
    dw_up = contract_dims(x_one_b, dupper_b, 0, 0)
    db_up = jnp.sum(dupper, axis=0)
    dx_one = dz_two + contract_dims(dupper_b, wu_back, 1, 1)
    dg_one = jnp.sum(dx_one * n_one, axis=0)
    db_one = jnp.sum(dx_one, axis=0)
    dz_one = norm_back(dx_one * g1, n_one, rstd_one)
    dz_one_b = dz_one.astype(bf16)
    dw_out = contract_dims(context_b_t, dz_one_b, 1, 0)
    db_out = jnp.sum(dz_one, axis=0)
    dctx_t = contract_dims(wo_back, dz_one_b, 1, 1)
    dctx_b_t = dctx_t.astype(bf16)
    delta = jnp.sum(heads_first(dctx_t) * ctx_heads, axis=1)
    qh = heads_first(query_t)

    def head_bwd(operations):
        query_index, key_index, value_index, lse_index, context_grad_index, delta_index = operations
        scores = contract_dims(query_index, key_index, 0, 0) * scale
        scores = jnp.where(valid[None, :], scores, -1e30)
        prob = jnp.exp(scores - lse_index[:, None])
        block_probs = prob.astype(bf16)
        value_gradient = contract_dims(context_grad_index, block_probs, 1, 0)
        prob_gradient = contract_dims(context_grad_index, value_index, 0, 0)
        dscore = (prob * (prob_gradient - delta_index[:, None])).astype(bf16)
        query_gradient = contract_dims(key_index, dscore, 1, 1) * scale
        key_gradient = contract_dims(query_index, dscore, 1, 0) * scale
        return (query_gradient, key_gradient, value_gradient)

    dqh, dkh, dvh = lax.map(
        head_bwd,
        (qh, heads_first(keys_b), heads_first(values_b), lse_all, heads_first(dctx_b_t), delta),
    )
    key_grad_t, value_grad_t = (
        lax.psum_scatter(
            dkh.reshape(width, -1).astype(jnp.bfloat16), "ctx", scatter_dimension=1, tiled=True
        ).astype(jnp.float32),
        lax.psum_scatter(
            dvh.reshape(width, -1).astype(jnp.bfloat16), "ctx", scatter_dimension=1, tiled=True
        ).astype(jnp.float32),
    )
    query_grad_t = dqh.reshape(width, -1)
    dqkv_b_t = jnp.concatenate([query_grad_t, key_grad_t, value_grad_t], axis=0).astype(bf16)
    dw_qkv = contract_dims(x, dqkv_b_t, 0, 1)
    dx = dz_one + contract_dims(dqkv_b_t, wq_back, 0, 1)
    grads = (
        dw_qkv,
        jnp.sum(query_grad_t, axis=1),
        jnp.sum(value_grad_t, axis=1),
        dw_out,
        db_out,
        dg_one,
        db_one,
        dw_up,
        db_up,
        dw_down,
        db_down,
        dg_two,
        db_two,
    )
    pieces = (
        lax.psum_scatter(
            grads[0].astype(jnp.bfloat16), "shard", scatter_dimension=0, tiled=True
        ).astype(jnp.float32),
        lax.psum_scatter(
            grads[1].astype(jnp.bfloat16), "shard", scatter_dimension=0, tiled=True
        ).astype(jnp.float32),
        lax.psum_scatter(
            grads[2].astype(jnp.bfloat16), "shard", scatter_dimension=0, tiled=True
        ).astype(jnp.float32),
        lax.psum_scatter(
            grads[3].astype(jnp.bfloat16), "shard", scatter_dimension=0, tiled=True
        ).astype(jnp.float32),
        lax.psum_scatter(
            grads[4].astype(jnp.bfloat16), "shard", scatter_dimension=0, tiled=True
        ).astype(jnp.float32),
        lax.psum_scatter(
            grads[5].astype(jnp.bfloat16), "shard", scatter_dimension=0, tiled=True
        ).astype(jnp.float32),
        lax.psum_scatter(
            grads[6].astype(jnp.bfloat16), "shard", scatter_dimension=0, tiled=True
        ).astype(jnp.float32),
        lax.psum_scatter(
            grads[7].astype(jnp.bfloat16), "shard", scatter_dimension=0, tiled=True
        ).astype(jnp.float32),
        lax.psum_scatter(
            grads[8].astype(jnp.bfloat16), "shard", scatter_dimension=0, tiled=True
        ).astype(jnp.float32),
        lax.psum_scatter(
            grads[9].astype(jnp.bfloat16), "shard", scatter_dimension=0, tiled=True
        ).astype(jnp.float32),
        lax.psum_scatter(
            grads[10].astype(jnp.bfloat16), "shard", scatter_dimension=0, tiled=True
        ).astype(jnp.float32),
        lax.psum_scatter(
            grads[11].astype(jnp.bfloat16), "shard", scatter_dimension=0, tiled=True
        ).astype(jnp.float32),
        lax.psum_scatter(
            grads[12].astype(jnp.bfloat16), "shard", scatter_dimension=0, tiled=True
        ).astype(jnp.float32),
    )
    summed = (
        lax.psum(pieces[0].astype(jnp.bfloat16), "ctx").astype(jnp.float32),
        lax.psum(pieces[1].astype(jnp.bfloat16), "ctx").astype(jnp.float32),
        lax.psum(pieces[2].astype(jnp.bfloat16), "ctx").astype(jnp.float32),
        lax.psum(pieces[3].astype(jnp.bfloat16), "ctx").astype(jnp.float32),
        lax.psum(pieces[4].astype(jnp.bfloat16), "ctx").astype(jnp.float32),
        lax.psum(pieces[5].astype(jnp.bfloat16), "ctx").astype(jnp.float32),
        lax.psum(pieces[6].astype(jnp.bfloat16), "ctx").astype(jnp.float32),
        lax.psum(pieces[7].astype(jnp.bfloat16), "ctx").astype(jnp.float32),
        lax.psum(pieces[8].astype(jnp.bfloat16), "ctx").astype(jnp.float32),
        lax.psum(pieces[9].astype(jnp.bfloat16), "ctx").astype(jnp.float32),
        lax.psum(pieces[10].astype(jnp.bfloat16), "ctx").astype(jnp.float32),
        lax.psum(pieces[11].astype(jnp.bfloat16), "ctx").astype(jnp.float32),
        lax.psum(pieces[12].astype(jnp.bfloat16), "ctx").astype(jnp.float32),
    )
    return (
        out[None],
        dx[None],
        summed[0],
        summed[1],
        summed[2],
        summed[3],
        summed[4],
        summed[5],
        summed[6],
        summed[7],
        summed[8],
        summed[9],
        summed[10],
        summed[11],
        summed[12],
    )


def solution(mesh):
    in_specs = (
        P("shard", "ctx", None),
        P("shard"),
        P("shard", "ctx", None),
        P("shard", None),
        P("shard"),
        P("shard"),
        P("shard", None),
        P("shard"),
        P("shard"),
        P("shard"),
        P("shard", None),
        P("shard"),
        P("shard", None),
        P("shard"),
        P("shard"),
        P("shard"),
    )
    out_specs = (
        P("shard", "ctx", None),
        P("shard", "ctx", None),
        P("shard", None),
        P("shard"),
        P("shard"),
        P("shard", None),
        P("shard"),
        P("shard"),
        P("shard"),
        P("shard", None),
        P("shard"),
        P("shard", None),
        P("shard"),
        P("shard"),
        P("shard"),
    )
    return jax.shard_map(local, mesh=mesh, in_specs=in_specs, out_specs=out_specs, check_vma=False)
```

profile of v0, /device:TPU:0, one launch (start us, length us, event | category | flops | bytes accessed | tf_op | source)
XLA Modules:
  0.0 760.2 jit_solution(821553112586905481)
XLA Ops:
  15.8 18.3 %all-reduce.20 = (bf16[768]{0:T(1024)(128)(2,1)S(1)}, bf16[768]{0:T(1024)(128)(2,1)S(1)}, bf16[768]{0:T(1024)(128)(2,1)S(1)}, bf16[768]{0:T(1024)(128)(2,1)S(1)}...) all-reduce(bf16[768]{0:T(1024)(128)(2,1)S(1)} %dynamic-update-slice, ...), channel_id=1, replica_groups=mesh['shard'=4,'ctx'=8] {'shard'}, use_global_device_ids=true, to_apply=%add.1 | all-reduce | flops 5376 | bytes 21504
  34.1 25.7 %all-gather.8.cloned.1.call-done = bf16[768,2304]{1,0:T(8,128)(2,1)} async-done(((bf16[192,2304]{1,0:T(8,128)(2,1)}), bf16[768,2304]{1,0:T(8,128)(2,1)}) %all-gather.8.cloned.1.call-update) | async-done | bytes 3538960 | tf_op jit(solution)/shard_map/all_gather | solution.py:60
  66.6 8.3 %all-gather = bf16[4,1,768]{2,1,0:T(2,128)(2,1)S(1)} all-gather(bf16[1,1,768]{2,1,0:T(2,128)(2,1)S(1)} %reshape.174), channel_id=1, replica_groups=mesh['shard'=4,'ctx'=8] {'shard'}, dimensions={0}, use_global_device_ids=true | all-gather | bytes 7680 | tf_op jit(solution)/shard_map/all_gather | solution.py:68
  74.9 16.2 %all-gather.10.cloned.1.call-done = bf16[768,1024]{1,0:T(8,128)(2,1)} async-done(((bf16[768,128]{1,0:T(8,128)(2,1)}), bf16[768,1024]{1,0:T(8,128)(2,1)}) %all-gather.10.cloned.1.call-update) | async-done | bytes 1572880 | tf_op jit(solution)/shard_map/all_gather | solution.py:101
  91.2 28.1 %all-gather.12.cloned.1.call-done = bf16[768,1024]{1,0:T(8,128)(2,1)} async-done(((bf16[768,128]{1,0:T(8,128)(2,1)}), bf16[768,1024]{1,0:T(8,128)(2,1)}) %all-gather.12.cloned.1.call-update) | async-done | bytes 1572880 | tf_op jit(solution)/shard_map/all_gather | solution.py:100
  119.3 55.8 %while.28 = (s32[]{:T(128)}, f32[12,64,128]{2,1,0:T(8,128)S(1)}, f32[12,128]{1,0:T(8,128)}, bf16[12,64,1024]{2,1,0:T(8,128)(2,1)}, bf16[12,64,128]{2,1,0:T(8,128...) while((s32[]{:T(128)}, f32[12,64,128]{2,1,0:T(8,128)S(1)}, ...), condition=%wide.region_3.4_spmd.clone, body=%wide.region_0.3_spmd.clone.sunk | while | flops 34472832 | bytes 1892965 | solution.py:115
  177.2 28.8 %all-gather.16.cloned.1.call-done = bf16[768,3072]{1,0:T(8,128)(2,1)} async-done(((bf16[192,3072]{1,0:T(8,128)(2,1)}), bf16[768,3072]{1,0:T(8,128)(2,1)}) %all-gather.16.cloned.1.call-update) | async-done | bytes 4718608 | tf_op jit(solution)/shard_map/all_gather | solution.py:67
  206.0 7.6 %multiply_convert_fusion = (bf16[128,3072]{1,0:T(8,128)(2,1)S(1)}, f32[128,3072]{1,0:T(8,128)}) fusion(f32[3072]{0:T(1024)S(1)} %bitcast.162, bf16[768,3072]{1,0:T(8,128)(2,1)} %all-gather.16.cloned.1.call-done, f32[128,768]{1,0:T(8,128)S(1)} %get-tuple-element.303, f32[768]{0:T(1024)S(1)} %convert_element_type.209, f32[768]{0:T(1024)S(1)} %convert_element_type.208, ...), kind=kOutput, calls=%fused_computation.67 | convolution fusion | flops 630423552 | bytes 7490560 | tf_op jit(solution)/shard_map/dot_general | solution.py:123
  213.7 51.0 %all-gather.18.cloned.1.call-done = bf16[3072,768]{1,0:T(8,128)(2,1)} async-done(((bf16[768,768]{1,0:T(8,128)(2,1)}), bf16[3072,768]{1,0:T(8,128)(2,1)}) %all-gather.18.cloned.1.call-update) | async-done | bytes 4718608 | tf_op jit(solution)/shard_map/all_gather | solution.py:69
  264.7 3.4 fusion.91
  269.9 5.5 fusion.93
  286.0 87.0 %while.29 = (s32[]{:T(128)}, f32[12,64,128]{2,1,0:T(8,128)S(1)}, bf16[12,64,1024]{2,1,0:T(8,128)(2,1)}, bf16[12,64,1024]{2,1,0:T(8,128)(2,1)}, bf16[12,64,1024]{...) while((s32[]{:T(128)}, f32[12,64,128]{2,1,0:T(8,128)S(1)}, ...), condition=%wide.region_14.15_spmd.clone, body=%wide.region_13.14_spmd.clone.sunk | while | flops 84878336 | bytes 3385469 | solution.py:168
  379.3 30.6 %reduce-scatter.19.cloned.1.call-done = bf16[128,768]{1,0:T(8,128)(2,1)} async-done(((bf16[1024,768]{1,0:T(8,128)(2,1)}), bf16[128,768]{1,0:T(8,128)(2,1)}) %reduce-scatter.19.cloned.1.call-update) | async-done | bytes 196624
  411.0 34.3 %reduce-scatter.21.cloned.1.call-done = bf16[128,768]{1,0:T(8,128)(2,1)} async-done(((bf16[1024,768]{1,0:T(8,128)(2,1)}), bf16[128,768]{1,0:T(8,128)(2,1)}) %reduce-scatter.21.cloned.1.call-update) | async-done | bytes 196624
  449.3 5.8 copy.44
  457.6 3.7 convolution_convert_fusion.1
  461.3 3.6 convolution_convert_fusion
  465.0 35.7 %reduce-scatter.23.cloned.1.call-done = bf16[192,2304]{1,0:T(8,128)(2,1)} async-done(((bf16[768,2304]{1,0:T(8,128)(2,1)}), bf16[192,2304]{1,0:T(8,128)(2,1)}) %reduce-scatter.23.cloned.1.call-update) | async-done | bytes 884752
  503.0 29.7 %reduce-scatter.13.cloned.1.call-done = bf16[192,768]{1,0:T(8,128)(2,1)} async-done(((bf16[768,768]{1,0:T(8,128)(2,1)}), bf16[192,768]{1,0:T(8,128)(2,1)}) %reduce-scatter.13.cloned.1.call-update) | async-done | bytes 294928 | tf_op jit(solution)/shard_map/reduce_scatter | solution.py:209
  532.8 60.0 %reduce-scatter.15.cloned.1.call-done = bf16[192,3072]{1,0:T(8,128)(2,1)} async-done(((bf16[768,3072]{1,0:T(8,128)(2,1)}), bf16[192,3072]{1,0:T(8,128)(2,1)}) %reduce-scatter.15.cloned.1.call-update) | async-done | bytes 1179664 | tf_op jit(solution)/shard_map/reduce_scatter | solution.py:221
  592.8 59.8 %reduce-scatter.17.cloned.1.call-done = bf16[768,768]{1,0:T(8,128)(2,1)} async-done(((bf16[3072,768]{1,0:T(8,128)(2,1)}), bf16[768,768]{1,0:T(8,128)(2,1)}) %reduce-scatter.17.cloned.1.call-update) | async-done | bytes 1179664 | tf_op jit(solution)/shard_map/reduce_scatter | solution.py:227
  659.2 16.7 %all-reduce.19 = (bf16[768]{0:T(1024)(128)(2,1)}, bf16[768]{0:T(1024)(128)(2,1)}, bf16[768]{0:T(1024)(128)(2,1)}, bf16[768]{0:T(1024)(128)(2,1)}, bf16[768]{0:T(...) all-reduce(bf16[768]{0:T(1024)(128)(2,1)} %dynamic-update-slice.7, ...), channel_id=1, replica_groups=mesh['shard'=4,'ctx'=8] {'shard'}, use_global_device_ids=true, to_apply=%add.7 | all-reduce | flops 9984 | bytes 39936
  686.7 15.6 %all-reduce.17 = (bf16[192]{0:T(256)(128)(2,1)}, bf16[192]{0:T(256)(128)(2,1)}, bf16[192]{0:T(256)(128)(2,1)}, bf16[192]{0:T(256)(128)(2,1)}, bf16[192]{0:T(256)...) all-reduce(bf16[192]{0:T(256)(128)(2,1)} %dynamic-slice.9, ...), channel_id=1, replica_groups=mesh['shard'=4,'ctx'=8] {'ctx'}, use_global_device_ids=true, to_apply=%region_21.22 | all-reduce | flops 2304 | bytes 9216 | tf_op jit(solution)/shard_map/psum | solution.py:242
  718.3 28.3 %all-reduce.23.cloned.1.call-done = (bf16[192,2304]{0,1:T(8,128)(2,1)}, bf16[192,768]{1,0:T(8,128)(2,1)}, bf16[192,3072]{1,0:T(8,128)(2,1)}, bf16[768,768]{1,0:T(8,128)(2,1)}) async-done(((bf16[192,2304]{0,1:T(8,128)(2,1)}, bf16[192,768]{1,0:T(8,128)(2,1)}, bf16[192,3072]{1,0:T(8,128)(2,1)}, bf16[768,768]{1,0:T(8,128)(2,1)}), (bf16[192,2304]{0,1:T(8,128)(2,1)}, bf16[192,768]{1,0:T(8,128)(2,1)}, ...) | async-done | bytes 3538960 | tf_op jit(solution)/shard_map/psum | solution.py:241
  (325 shorter events, 226.3 us)
Async XLA Ops:
  7.2 52.7 %all-gather.8.cloned.1.call-start = ((), (), s32[]{:S(2)}) async-start(), calls=%async_computation.6 | async-start | bytes 4423680 | tf_op jit(solution)/shard_map/all_gather | solution.py:60
  7.9 83.3 %all-gather.10.cloned.1.call-start = ((), (), s32[]{:S(2)}) async-start(), calls=%async_computation.7 | async-start | bytes 1769472 | tf_op jit(solution)/shard_map/all_gather | solution.py:101
  63.9 55.3 %all-gather.12.cloned.1.call-start = ((), (), s32[]{:S(2)}) async-start(), calls=%async_computation.8 | async-start | bytes 1769472 | tf_op jit(solution)/shard_map/all_gather | solution.py:100
  64.7 110.5 %all-gather.14.cloned.1.call-start = ((), (), s32[]{:S(2)}) async-start(), calls=%async_computation.9 | async-start | bytes 1474560 | tf_op jit(solution)/shard_map/all_gather | solution.py:63
  65.3 140.8 %all-gather.16.cloned.1.call-start = ((), (), s32[]{:S(2)}) async-start(), calls=%async_computation.10 | async-start | bytes 5898240 | tf_op jit(solution)/shard_map/all_gather | solution.py:67
  65.9 198.8 %all-gather.18.cloned.1.call-start = ((), (), s32[]{:S(2)}) async-start(), calls=%async_computation.11 | async-start | bytes 5898240 | tf_op jit(solution)/shard_map/all_gather | solution.py:69
  66.5 343.5 %reduce-scatter.19.cloned.1.call-start = ((), (), s32[]{:S(2)}) async-start(), calls=%async_computation.15 | async-start | bytes 1769472
  119.3 55.9 %copy-start.5 = (bf16[1,128,768]{2,1,0:T(8,128)(2,1)S(1)}, bf16[1,128,768]{2,1,0:T(8,128)(2,1)}, u32[]{:S(2)}) copy-start(bf16[1,128,768]{2,1,0:T(8,128)(2,1)} %param.20) | copy-start | bytes 589828
  175.2 38.5 %copy-start.9 = (bf16[12,64,128]{2,1,0:T(8,128)(2,1)}, bf16[12,64,128]{2,1,0:T(8,128)(2,1)S(1)}, u32[]{:S(2)}) copy-start(bf16[12,64,128]{2,1,0:T(8,128)(2,1)S(1)} %convert_element_type.205) | copy-start | bytes 589828
  177.2 98.2 %copy-start.16 = (f32[128]{0:T(128)}, f32[128]{0:T(128)S(1)}, u32[]{:S(2)}) copy-start(f32[128]{0:T(128)S(1)} %add_rsqrt_fusion.1) | copy-start | bytes 1540
  268.1 7.3 copy-start.18
  268.3 7.1 copy-start.21
  279.3 175.9 %copy-start.2 = (f32[128,768]{1,0:T(8,128)}, f32[128,768]{1,0:T(8,128)S(1)}, u32[]{:S(2)}) copy-start(f32[128,768]{1,0:T(8,128)S(1)} %get-tuple-element.291) | copy-start | bytes 1179652
  375.6 69.7 %reduce-scatter.21.cloned.1.call-start = ((), (), s32[]{:S(2)}) async-start(), calls=%async_computation.16 | async-start | bytes 1769472
  378.3 122.4 %reduce-scatter.23.cloned.1.call-start = ((), (), s32[]{:S(2)}) async-start(), calls=%async_computation.17 | async-start | bytes 4423680
  379.3 70.0 %copy-start.8 = (bf16[12,64,128]{2,1,0:T(8,128)(2,1)}, bf16[12,64,128]{2,1,0:T(8,128)(2,1)S(1)}, u32[]{:S(2)}) copy-start(bf16[12,64,128]{2,1,0:T(8,128)(2,1)S(1)} %get-tuple-element.298) | copy-start | bytes 589828
  411.0 38.3 %copy-start.6 = (bf16[768,128]{1,0:T(8,128)(2,1)}, bf16[768,128]{1,0:T(8,128)(2,1)S(1)}, u32[]{:S(2)}) copy-start(bf16[768,128]{1,0:T(8,128)(2,1)S(1)} %copy.41) | copy-start | bytes 589828
  455.1 77.6 %reduce-scatter.13.cloned.1.call-start = ((), (), s32[]{:S(2)}) async-start(), calls=%async_computation.12 | async-start | bytes 1474560 | tf_op jit(solution)/shard_map/reduce_scatter | solution.py:209
  457.5 135.3 %reduce-scatter.15.cloned.1.call-start = ((), (), s32[]{:S(2)}) async-start(), calls=%async_computation.13 | async-start | bytes 5898240 | tf_op jit(solution)/shard_map/reduce_scatter | solution.py:221
  461.3 191.4 %reduce-scatter.17.cloned.1.call-start = ((), (), s32[]{:S(2)}) async-start(), calls=%async_computation.14 | async-start | bytes 5898240 | tf_op jit(solution)/shard_map/reduce_scatter | solution.py:227
  464.9 281.7 %all-reduce.23.cloned.1.call-start = ((), (), s32[]{:S(2)}) async-start(), calls=%async_computation.18 | async-start | bytes 7667712 | tf_op jit(solution)/shard_map/psum | solution.py:241
  652.6 6.6 copy-start.20
  652.6 60.5 %copy-start.19 = (f32[128]{0:T(128)S(1)}, f32[128]{0:T(128)}, u32[]{:S(2)}) copy-start(f32[128]{0:T(128)} %copy-done.18) | copy-start | bytes 1540
  652.6 62.3 %copy-start = (bf16[768,2304]{1,0:T(8,128)(2,1)S(1)}, bf16[768,2304]{1,0:T(8,128)(2,1)}, u32[]{:S(2)}) copy-start(bf16[768,2304]{1,0:T(8,128)(2,1)} %all-gather.8.cloned.1.call-done) | copy-start | bytes 10616836
  (15 other events, 45.1 us)
Sparse Core Ops, SparseCore 0:
  9.8 49.9 all-gather.7
  64.0 27.0 all-gather.9
  93.3 25.8 all-gather.11
  121.0 26.3 all-gather.13
  149.1 56.9 all-gather.15
  207.7 56.9 all-gather.17
  375.7 34.1 reduce-scatter.18
  412.8 32.5 reduce-scatter.20
  455.2 45.4 reduce-scatter.22
  504.1 28.6 reduce-scatter.12
  535.8 56.9 reduce-scatter.14
  595.6 56.9 reduce-scatter.16
  655.8 90.7 all-reduce.22
where the time goes:
time: 764 us; the launch traced here: 760 us
  waiting for transfers between devices  431 us (56%)
  matrix products  140 us (18%)
  local copies, waits for them, and re-layouts  66.7 us (9%)
  blocking collectives  58.9 us (8%)
  other arithmetic  46.2 us (6%)
  between operations  16.2 us (2%)
    dot_general x94, matrix products, contract_dims(): lax.dot_general(left, right, (((left_dim,), (right_dim,)), ((), ())), pre...  129 us
    unnamed x16, waiting for transfers between devices  103 us
    reduce_scatter x1, waiting for transfers between devices, local(): lax.psum_scatter(grads[7].astype(jnp.bfloat16), 'shard', scatter_dimensio...  60 us
    reduce_scatter x1, waiting for transfers between devices, local(): lax.psum_scatter(grads[9].astype(jnp.bfloat16), 'shard', scatter_dimensio...  59.8 us
    all_gather x1, waiting for transfers between devices, local(): lax.all_gather(w_down, 'shard', axis=0, tiled=True)  51 us
    unnamed x86, local copies, waits for them, and re-layouts  37.9 us
    unnamed x2, blocking collectives  35 us
    reduce_scatter x1, waiting for transfers between devices, local(): lax.psum_scatter(grads[3].astype(jnp.bfloat16), 'shard', scatter_dimensio...  29.7 us
  transfers between devices with their start and end apart: 13, of which 12 were waited for; matrix products, arithmetic and copies ran while one was open for 16% of the time, Pallas kernels for 0%

commit v1 on v0

--- a/solution.py
+++ b/solution.py
@@ -6,6 +6,14 @@
 
 HEADS = 12
 EPS = 1e-06
+
+
+def _define_column(mine_x, dim_at):
+    mine_x = jnp.moveaxis(mine_x, 0, dim_at)
+    mat_out = mine_x.shape
+    return mine_x.reshape(
+        *mat_out[:dim_at], mat_out[dim_at] * mat_out[dim_at + 1], *mat_out[dim_at + 2 :]
+    )
 
 
 def normalize(z):
@@ -56,6 +64,17 @@
 ):
     single_float = jnp.float32
     bf16 = jnp.bfloat16
+
+    def expand_copies(load, net_axis, join_dim):
+        how_many = lax.axis_size(net_axis)
+        cards = [(m, (m + 1) % how_many) for m in range(how_many)]
+        store = [load]
+        while len(store) < how_many:
+            store.append(lax.ppermute(store[-1], net_axis, cards))
+        x_new = lax.axis_index(net_axis)
+        store = jnp.stack(store)[(x_new - jnp.arange(how_many)) % how_many]
+        return _define_column(store, join_dim)
+
     full = (
         lax.all_gather(w_qkv, "shard", axis=0, tiled=True),
         lax.all_gather(b_query, "shard", axis=0, tiled=True),
@@ -66,7 +85,7 @@
         lax.all_gather(ln1_bias, "shard", axis=0, tiled=True),
         lax.all_gather(w_up, "shard", axis=0, tiled=True),
         lax.all_gather(b_up, "shard", axis=0, tiled=True),
-        lax.all_gather(w_down, "shard", axis=0, tiled=True),
+        expand_copies(w_down, "shard", 0),
         lax.all_gather(b_down, "shard", axis=0, tiled=True),
         lax.all_gather(ln2_gain, "shard", axis=0, tiled=True),
         lax.all_gather(ln2_bias, "shard", axis=0, tiled=True),

time: 764 us -> 738 us (0.966)
  waiting for transfers between devices: 431 us -> 359 us
  blocking collectives: 58.9 us -> 80.9 us
    ppermute x0 -> x3, waiting for transfers between devices: none -> 53.9 us  [expand_copies(): store.append(lax.ppermute(store[-1], net_axis, cards))]
    all_gather x1 -> x0, waiting for transfers between devices: 51 us -> none  [local(): lax.all_gather(w_down, 'shard', axis=0, tiled=True)]
    all_gather x1, waiting for transfers between devices: 28.8 us -> 0.43 us  [local(): lax.all_gather(w_up, 'shard', axis=0, tiled=True)]
    all_gather x1, waiting for transfers between devices: 28.1 us -> 0.01 us  [local(): lax.all_gather(keys_t, 'ctx', axis=1, tiled=True)]
    all_gather x1, blocking collectives: 8.3 us -> 29.7 us  [local(): lax.all_gather(b_up, 'shard', axis=0, tiled=True)]
    all_gather x1, waiting for transfers between devices: 16.2 us -> 0.01 us  [local(): lax.all_gather(values_t, 'ctx', axis=1, tiled=True)]
    dot_general x94, matrix products: 129 us -> 139 us  [contract_dims(): lax.dot_general(left, right, (((left_dim,), (right_dim,)), ((), ())), pre...]
    unnamed x16 -> x15, waiting for transfers between devices: 103 us -> 102 us
  transfers between devices with their start and end apart: 13 -> 15, of which waited for: 12 -> 11; matrix products, arithmetic and copies ran while one was open for 16% -> 17% of each run, Pallas kernels for 0% -> 0%
where the time goes in v1:
time: 738 us; the launch traced here: 730 us
  waiting for transfers between devices  359 us (49%)
  matrix products  146 us (20%)
  blocking collectives  80.9 us (11%)
  local copies, waits for them, and re-layouts  73.3 us (10%)
  other arithmetic  51.3 us (7%)
  between operations  16.5 us (2%)
    dot_general x94, matrix products, contract_dims(): lax.dot_general(left, right, (((left_dim,), (right_dim,)), ((), ())), pre...  139 us
    unnamed x15, waiting for transfers between devices  102 us
    reduce_scatter x1, waiting for transfers between devices, local(): lax.psum_scatter(grads[9].astype(jnp.bfloat16), 'shard', scatter_dimensio...  60 us
    reduce_scatter x1, waiting for transfers between devices, local(): lax.psum_scatter(grads[7].astype(jnp.bfloat16), 'shard', scatter_dimensio...  59.9 us
    ppermute x3, waiting for transfers between devices, expand_copies(): store.append(lax.ppermute(store[-1], net_axis, cards))  53.9 us
    unnamed x82, local copies, waits for them, and re-layouts  39.1 us
    unnamed x2, blocking collectives  35.6 us
    reduce_scatter x1, waiting for transfers between devices, local(): lax.psum_scatter(grads[3].astype(jnp.bfloat16), 'shard', scatter_dimensio...  29.9 us
  transfers between devices with their start and end apart: 15, of which 11 were waited for; matrix products, arithmetic and copies ran while one was open for 17% of the time, Pallas kernels for 0%

profile of v1, /device:TPU:0, one launch (start us, length us, event | category | flops | bytes accessed | tf_op | source)
XLA Modules:
  0.0 730.1 jit_solution(4998123526281980113)
XLA Ops:
  15.8 18.9 %all-reduce.20 = (bf16[768]{0:T(1024)(128)(2,1)S(1)}, bf16[768]{0:T(1024)(128)(2,1)S(1)}, bf16[768]{0:T(1024)(128)(2,1)S(1)}, bf16[768]{0:T(1024)(128)(2,1)S(1)}...) all-reduce(bf16[768]{0:T(1024)(128)(2,1)S(1)} %dynamic-update-slice, ...), channel_id=1, replica_groups=mesh['shard'=4,'ctx'=8] {'shard'}, use_global_device_ids=true, to_apply=%add.1 | all-reduce | flops 5376 | bytes 21504
  34.7 25.1 %all-gather.7.cloned.1.call-done = bf16[768,2304]{1,0:T(8,128)(2,1)} async-done(((bf16[192,2304]{1,0:T(8,128)(2,1)}), bf16[768,2304]{1,0:T(8,128)(2,1)}) %all-gather.7.cloned.1.call-update) | async-done | bytes 3538960 | tf_op jit(solution)/shard_map/all_gather | solution.py:79
  66.4 27.0 %collective-permute-done = bf16[768,768]{1,0:T(8,128)(2,1)S(1)} collective-permute-done((bf16[768,768]{1,0:T(8,128)(2,1)S(1)}, bf16[768,768]{1,0:T(8,128)(2,1)S(1)}, u32[]{:S(2)}, u32[]{:S(2)}) %collective-permute-start) | collective-permute-done | bytes 1179680 | tf_op jit(solution)/shard_map/ppermute | solution.py:73
  94.0 26.9 %collective-permute-done.1 = bf16[768,768]{1,0:T(8,128)(2,1)S(1)} collective-permute-done((bf16[768,768]{1,0:T(8,128)(2,1)S(1)}, bf16[768,768]{1,0:T(8,128)(2,1)S(1)}, u32[]{:S(2)}, u32[]{:S(2)}) %collective-permute-start.1) | collective-permute-done | bytes 1179680 | tf_op jit(solution)/shard_map/ppermute | solution.py:73
  122.3 29.7 %all-gather = bf16[4,1,768]{2,1,0:T(2,128)(2,1)S(1)} all-gather(bf16[1,1,768]{2,1,0:T(2,128)(2,1)S(1)} %reshape.235), channel_id=1, replica_groups=mesh['shard'=4,'ctx'=8] {'shard'}, dimensions={0}, use_global_device_ids=true | all-gather | bytes 7680 | tf_op jit(solution)/shard_map/all_gather | solution.py:87
  154.0 3.6 pad_maximum_fusion
  157.5 5.5 gather_fusion
  163.1 56.0 %while.28 = (s32[]{:T(128)}, f32[12,64,128]{2,1,0:T(8,128)S(1)}, f32[12,128]{1,0:T(8,128)}, bf16[12,64,1024]{2,1,0:T(8,128)(2,1)}, bf16[12,64,128]{2,1,0:T(8,128...) while((s32[]{:T(128)}, f32[12,64,128]{2,1,0:T(8,128)S(1)}, ...), condition=%wide.region_3.4_spmd.clone, body=%wide.region_0.3_spmd.clone.sunk | while | flops 34472832 | bytes 1892965 | solution.py:134
  221.6 6.0 multiply_convert_fusion
  230.4 5.5 fusion.95
  245.6 95.7 %while.29 = (s32[]{:T(128)}, f32[12,64,128]{2,1,0:T(8,128)S(1)}, bf16[12,64,1024]{2,1,0:T(8,128)(2,1)}, bf16[12,64,1024]{2,1,0:T(8,128)(2,1)}, bf16[12,64,1024]{...) while((s32[]{:T(128)}, f32[12,64,128]{2,1,0:T(8,128)S(1)}, ...), condition=%wide.region_14.15_spmd.clone, body=%wide.region_13.14_spmd.clone.sunk | while | flops 84878336 | bytes 3385469 | solution.py:187
  347.4 30.9 %reduce-scatter.19.cloned.1.call-done = bf16[128,768]{1,0:T(8,128)(2,1)} async-done(((bf16[1024,768]{1,0:T(8,128)(2,1)}), bf16[128,768]{1,0:T(8,128)(2,1)}) %reduce-scatter.19.cloned.1.call-update) | async-done | bytes 196624
  379.4 34.4 %reduce-scatter.21.cloned.1.call-done = bf16[128,768]{1,0:T(8,128)(2,1)} async-done(((bf16[1024,768]{1,0:T(8,128)(2,1)}), bf16[128,768]{1,0:T(8,128)(2,1)}) %reduce-scatter.21.cloned.1.call-update) | async-done | bytes 196624
  414.9 3.8 fusion.47
  418.7 5.8 copy.44
  427.2 3.6 convolution_convert_fusion.1
  430.9 3.6 convolution_convert_fusion
  434.6 35.6 %reduce-scatter.23.cloned.1.call-done = bf16[192,2304]{1,0:T(8,128)(2,1)} async-done(((bf16[768,2304]{1,0:T(8,128)(2,1)}), bf16[192,2304]{1,0:T(8,128)(2,1)}) %reduce-scatter.23.cloned.1.call-update) | async-done | bytes 884752
  472.5 29.9 %reduce-scatter.13.cloned.1.call-done = bf16[192,768]{1,0:T(8,128)(2,1)} async-done(((bf16[768,768]{1,0:T(8,128)(2,1)}), bf16[192,768]{1,0:T(8,128)(2,1)}) %reduce-scatter.13.cloned.1.call-update) | async-done | bytes 294928 | tf_op jit(solution)/shard_map/reduce_scatter | solution.py:228
  502.5 59.9 %reduce-scatter.15.cloned.1.call-done = bf16[192,3072]{1,0:T(8,128)(2,1)} async-done(((bf16[768,3072]{1,0:T(8,128)(2,1)}), bf16[192,3072]{1,0:T(8,128)(2,1)}) %reduce-scatter.15.cloned.1.call-update) | async-done | bytes 1179664 | tf_op jit(solution)/shard_map/reduce_scatter | solution.py:240
  562.3 60.0 %reduce-scatter.17.cloned.1.call-done = bf16[768,768]{1,0:T(8,128)(2,1)} async-done(((bf16[3072,768]{1,0:T(8,128)(2,1)}), bf16[768,768]{1,0:T(8,128)(2,1)}) %reduce-scatter.17.cloned.1.call-update) | async-done | bytes 1179664 | tf_op jit(solution)/shard_map/reduce_scatter | solution.py:246
  628.9 16.7 %all-reduce.19 = (bf16[768]{0:T(1024)(128)(2,1)}, bf16[768]{0:T(1024)(128)(2,1)}, bf16[768]{0:T(1024)(128)(2,1)}, bf16[768]{0:T(1024)(128)(2,1)}, bf16[768]{0:T(...) all-reduce(bf16[768]{0:T(1024)(128)(2,1)} %dynamic-update-slice.7, ...), channel_id=1, replica_groups=mesh['shard'=4,'ctx'=8] {'shard'}, use_global_device_ids=true, to_apply=%add.7 | all-reduce | flops 9984 | bytes 39936
  656.4 15.6 %all-reduce.17 = (bf16[192]{0:T(256)(128)(2,1)}, bf16[192]{0:T(256)(128)(2,1)}, bf16[192]{0:T(256)(128)(2,1)}, bf16[192]{0:T(256)(128)(2,1)}, bf16[192]{0:T(256)...) all-reduce(bf16[192]{0:T(256)(128)(2,1)} %dynamic-slice.9, ...), channel_id=1, replica_groups=mesh['shard'=4,'ctx'=8] {'ctx'}, use_global_device_ids=true, to_apply=%region_21.22 | all-reduce | flops 2304 | bytes 9216 | tf_op jit(solution)/shard_map/psum | solution.py:261
  688.2 28.0 %all-reduce.23.cloned.1.call-done = (bf16[192,2304]{0,1:T(8,128)(2,1)}, bf16[192,768]{1,0:T(8,128)(2,1)}, bf16[192,3072]{1,0:T(8,128)(2,1)}, bf16[768,768]{1,0:T(8,128)(2,1)}) async-done(((bf16[192,2304]{0,1:T(8,128)(2,1)}, bf16[192,768]{1,0:T(8,128)(2,1)}, bf16[192,3072]{1,0:T(8,128)(2,1)}, bf16[768,768]{1,0:T(8,128)(2,1)}), (bf16[192,2304]{0,1:T(8,128)(2,1)}, bf16[192,768]{1,0:T(8,128)(2,1)}, ...) | async-done | bytes 3538960 | tf_op jit(solution)/shard_map/psum | solution.py:260
  (329 shorter events, 236.8 us)
Async XLA Ops:
  7.2 52.7 %all-gather.7.cloned.1.call-start = ((), (), s32[]{:S(2)}) async-start(), calls=%async_computation.6 | async-start | bytes 4423680 | tf_op jit(solution)/shard_map/all_gather | solution.py:79
  7.9 155.1 %all-gather.9.cloned.1.call-start = ((), (), s32[]{:S(2)}) async-start(), calls=%async_computation.7 | async-start | bytes 1769472 | tf_op jit(solution)/shard_map/all_gather | solution.py:120
  64.0 99.0 %all-gather.11.cloned.1.call-start = ((), (), s32[]{:S(2)}) async-start(), calls=%async_computation.8 | async-start | bytes 1769472 | tf_op jit(solution)/shard_map/all_gather | solution.py:119
  64.8 154.4 %all-gather.13.cloned.1.call-start = ((), (), s32[]{:S(2)}) async-start(), calls=%async_computation.9 | async-start | bytes 1474560 | tf_op jit(solution)/shard_map/all_gather | solution.py:82
  64.9 28.5 %collective-permute-start = (bf16[768,768]{1,0:T(8,128)(2,1)S(1)}, bf16[768,768]{1,0:T(8,128)(2,1)S(1)}, u32[]{:S(2)}, u32[]{:S(2)}) collective-permute-start(bf16[768,768]{1,0:T(8,128)(2,1)S(1)} %copy-done.10), channel_id=1, source_target_pairs={{0,8},{8,16},{16,24},{24,0},{1,9},{9,17},{17,25},{25,1},{2,10},{10... | collective-permute-start | bytes 3538952 | tf_op jit(solution)/shard_map/ppermute | solution.py:73
  93.3 27.6 %collective-permute-start.1 = (bf16[768,768]{1,0:T(8,128)(2,1)S(1)}, bf16[768,768]{1,0:T(8,128)(2,1)S(1)}, u32[]{:S(2)}, u32[]{:S(2)}) collective-permute-start(bf16[768,768]{1,0:T(8,128)(2,1)S(1)} %collective-permute-done), channel_id=1, source_target_pairs={{0,8},{8,16},{16,24},{24,0},{1,9},{9,17},{17,25},{25,1},{2,10},{10... | collective-permute-start | bytes 3538952 | tf_op jit(solution)/shard_map/ppermute | solution.py:73
  93.9 127.7 %all-gather.15.cloned.1.call-start = ((), (), s32[]{:S(2)}) async-start(), calls=%async_computation.10 | async-start | bytes 5898240 | tf_op jit(solution)/shard_map/all_gather | solution.py:86
  120.9 33.0 %collective-permute-start.2 = (bf16[768,768]{1,0:T(8,128)(2,1)S(1)}, bf16[768,768]{1,0:T(8,128)(2,1)}, u32[]{:S(2)}, u32[]{:S(2)}) collective-permute-start(bf16[768,768]{1,0:T(8,128)(2,1)S(1)} %collective-permute-done.1), channel_id=1, source_target_pairs={{0,8},{8,16},{16,24},{24,0},{1,9},{9,17},{17,25},{25,1},{2,10},{10... | collective-permute-start | bytes 3538952 | tf_op jit(solution)/shard_map/ppermute | solution.py:73
  121.0 257.4 %reduce-scatter.19.cloned.1.call-start = ((), (), s32[]{:S(2)}) async-start(), calls=%async_computation.14 | async-start | bytes 1769472
  163.1 56.1 %copy-start.4 = (bf16[1,128,768]{2,1,0:T(8,128)(2,1)S(1)}, bf16[1,128,768]{2,1,0:T(8,128)(2,1)}, u32[]{:S(2)}) copy-start(bf16[1,128,768]{2,1,0:T(8,128)(2,1)} %param.20) | copy-start | bytes 589828
  163.1 56.1 %copy-start.14 = (f32[768]{0:T(1024)S(1)}, f32[768]{0:T(1024)}, u32[]{:S(2)}) copy-start(f32[768]{0:T(1024)} %convert_element_type.207) | copy-start | bytes 9220
  219.1 8.5 %copy-start.7 = (bf16[12,64,128]{2,1,0:T(8,128)(2,1)}, bf16[12,64,128]{2,1,0:T(8,128)(2,1)S(1)}, u32[]{:S(2)}) copy-start(bf16[12,64,128]{2,1,0:T(8,128)(2,1)S(1)} %convert_element_type.205) | copy-start | bytes 589828
  219.2 8.4 %slice-start = ((s8[4718592]{0:T(1024)(128)(4,1)}), s8[524288]{0:T(1024)(128)(4,1)S(1)}, s32[]{:S(2)}) async-start(s8[4718592]{0:T(1024)(128)(4,1)} %bitcast.151), calls=%async_computation.18 | async-start | bytes 1048576
  228.6 7.3 copy-start.16
  239.0 185.6 %copy-start.2 = (f32[128,768]{1,0:T(8,128)}, f32[128,768]{1,0:T(8,128)S(1)}, u32[]{:S(2)}) copy-start(f32[128,768]{1,0:T(8,128)S(1)} %get-tuple-element.291) | copy-start | bytes 1179652
  343.9 69.9 %reduce-scatter.21.cloned.1.call-start = ((), (), s32[]{:S(2)}) async-start(), calls=%async_computation.15 | async-start | bytes 1769472
  346.6 123.6 %reduce-scatter.23.cloned.1.call-start = ((), (), s32[]{:S(2)}) async-start(), calls=%async_computation.16 | async-start | bytes 4423680
  379.4 39.3 %copy-start.5 = (bf16[768,128]{1,0:T(8,128)(2,1)}, bf16[768,128]{1,0:T(8,128)(2,1)S(1)}, u32[]{:S(2)}) copy-start(bf16[768,128]{1,0:T(8,128)(2,1)S(1)} %copy.41) | copy-start | bytes 589828
  424.5 77.9 %reduce-scatter.13.cloned.1.call-start = ((), (), s32[]{:S(2)}) async-start(), calls=%async_computation.11 | async-start | bytes 1474560 | tf_op jit(solution)/shard_map/reduce_scatter | solution.py:228
  426.9 135.4 %reduce-scatter.15.cloned.1.call-start = ((), (), s32[]{:S(2)}) async-start(), calls=%async_computation.12 | async-start | bytes 5898240 | tf_op jit(solution)/shard_map/reduce_scatter | solution.py:240
  430.9 191.4 %reduce-scatter.17.cloned.1.call-start = ((), (), s32[]{:S(2)}) async-start(), calls=%async_computation.13 | async-start | bytes 5898240 | tf_op jit(solution)/shard_map/reduce_scatter | solution.py:246
  434.5 281.7 %all-reduce.23.cloned.1.call-start = ((), (), s32[]{:S(2)}) async-start(), calls=%async_computation.17 | async-start | bytes 7667712 | tf_op jit(solution)/shard_map/psum | solution.py:260
  622.3 60.8 %copy-start.17 = (f32[128]{0:T(128)S(1)}, f32[128]{0:T(128)}, u32[]{:S(2)}) copy-start(f32[128]{0:T(128)} %copy-done.16) | copy-start | bytes 1540
  622.3 62.6 %copy-start = (bf16[768,2304]{1,0:T(8,128)(2,1)S(1)}, bf16[768,2304]{1,0:T(8,128)(2,1)}, u32[]{:S(2)}) copy-start(bf16[768,2304]{1,0:T(8,128)(2,1)} %all-gather.7.cloned.1.call-done) | copy-start | bytes 10616836
  (15 other events, 50.3 us)
Sparse Core Ops, SparseCore 0:
  9.8 49.9 all-gather.6
  64.1 27.0 all-gather.8
  93.4 25.7 all-gather.10
  121.0 41.8 all-gather.12
  164.6 57.0 all-gather.14
  344.0 34.2 reduce-scatter.18
  381.2 32.5 reduce-scatter.20
  424.7 45.4 reduce-scatter.22
  473.7 28.7 reduce-scatter.12
  505.3 56.9 reduce-scatter.14
  565.3 56.9 reduce-scatter.16
  625.4 90.7 all-reduce.22
